TPU v7x, 32 devices: a whole 2x2x4 slice. The times are simulated.
32 devices in a mesh: dp: 8 (over z, x), mp: 4 (over y, core).
Axes of the slice: x: 2, y: 2, z: 4, core: 2. Of those that a mesh axis runs over, the one named last changes fastest.
Arguments:
- encoder_rows: bfloat16 [16384, 768], P('dp'), may hold values from -6 to 6
- piece_extent_sequence: int32 [32, 8], P('dp'), may hold values from 1 to 192, 512 in all within a row
- triple_projection_matrix: bfloat16 [3, 768, 768], P(None, None, 'mp'), may hold values from -0.21875 to 0.21875
- asker_content_shifts: float32 [2, 768], P(None, 'mp'), may hold values from -3 to 3
- mixing_result_matrix: bfloat16 [768, 768], P('mp'), may hold values from -1.75 to 1.75
- mixing_result_offset_vector: float32 [768], replicated, may hold values from -2 to 2
- mixing_normalizer_scale: float32 [768], replicated, may hold values from 0.25 to 1.75
- mixing_normalizer_shift: float32 [768], replicated, may hold values from -2 to 2
- widen_matrix: bfloat16 [768, 3072], P(None, 'mp'), may hold values from -0.21875 to 0.21875
- widen_shift_vector: float32 [3072], P('mp'), may hold values from -3 to 3
- narrow_matrix: bfloat16 [3072, 768], P('mp'), may hold values from -0.15625 to 0.15625
- narrow_shift_vector: float32 [768], replicated, may hold values from -2 to 2
- perceptron_normalizer_scale: float32 [768], replicated, may hold values from 0.25 to 1.75
- perceptron_normalizer_shift: float32 [768], replicated, may hold values from -2 to 2
- document_vectors: bfloat16 [131072, 768], P(('dp', 'mp')), may hold values from -0.36084392 to 0.36084392
- sharpness_factor: float32 [1], replicated, may hold values from 0.4 to 0.52
- correct_document_position: int32 [256], replicated, may hold values from 0 to 131071
- upstream_sensitivity: float32 [16384, 768], P('dp'), may hold values from -0.12 to 0.12
Outputs:
- layer_out: bfloat16 [16384, 768], P('dp')
- seg_loss: float32 [256], replicated
- grad_tokens: float32 [16384, 768], P('dp')
- grad_head_weight: float32 [3, 768, 768], P(None, None, 'mp')
- grad_head_bias: float32 [2, 768], P(None, 'mp')
- grad_out_weight: float32 [768, 768], P('mp')
- grad_out_bias: float32 [768], replicated
- grad_first_gain: float32 [768], replicated
- grad_first_shift: float32 [768], replicated
- grad_up_weight: float32 [768, 3072], P(None, 'mp')
- grad_up_bias: float32 [3072], P('mp')
- grad_down_weight: float32 [3072, 768], P('mp')
- grad_down_bias: float32 [768], replicated
- grad_second_gain: float32 [768], replicated
- grad_second_shift: float32 [768], replicated
- sharpness_derivative: float32 [1], replicated
Inputs may be any that keep to these rules, and one draw needn't show every extreme that they name: `piece_extent_sequence`: each row holds the lengths of the 8 segments of one block in order and sums to 512; the longest segment of each row has exactly 192 tokens.
All inputs are finite; a program needn't handle non-finite values.
Results may differ from a plain program's by a relative error of at most 0.013.
The roundings to bfloat16 on the way count: a program that leaves them out, or rounds other values in their place, can miss the bound.
Values may be sent and summed in bfloat16 or wider, within the bound.
A program may use at most 192 MiB of HBM per device.

v0:
```python
import jax
import jax.numpy as jnp
from jax import lax
from jax.sharding import PartitionSpec as P

HEAD = 64


norm_epsilon = 1e-05
masked_score = -1e30


def layer_norm(resid, gain, shift):
    centre = jnp.mean(resid, axis=-1, keepdims=True)
    centred = resid - centre
    spread = jnp.mean(centred * centred, axis=-1, keepdims=True)
    return centred * lax.rsqrt(spread + norm_epsilon) * gain + shift


def exact_gelu(values):
    return jax.nn.gelu(values, approximate=False)


def row_sums(part):
    return lax.psum(part, "mp")


def local(
    encoder_rows,
    piece_extent_sequence,
    triple_projection_matrix,
    asker_content_shifts,
    mixing_result_matrix,
    mixing_result_offset_vector,
    mixing_normalizer_scale,
    mixing_normalizer_shift,
    widen_matrix,
    widen_shift_vector,
    narrow_matrix,
    narrow_shift_vector,
    perceptron_normalizer_scale,
    perceptron_normalizer_shift,
    document_vectors,
    sharpness_factor,
    correct_document_position,
    upstream_sensitivity,
):
    single_float = jnp.float32
    brain_half_float = jnp.bfloat16
    highest = lax.Precision.HIGHEST
    nblock, nseg_block = piece_extent_sequence.shape
    rows = encoder_rows.shape[0]
    block = rows // nblock
    local_feat = triple_projection_matrix.shape[2]
    local_heads = local_feat // HEAD
    scale = HEAD ** (-0.5)
    ends = jnp.cumsum(piece_extent_sequence, axis=1)
    starts = ends - piece_extent_sequence
    places = jnp.arange(block, dtype=jnp.int32)
    seg_index = jnp.sum((places[None, :, None] >= ends[:, None, :]).astype(jnp.int32), axis=2)
    same_seg = (seg_index[:, :, None] == seg_index[:, None, :])[:, None]
    firsts = (jnp.arange(nblock, dtype=jnp.int32)[:, None] * block + starts).reshape(-1)
    select = firsts[:, None] == jnp.arange(rows, dtype=jnp.int32)[None, :]
    picker = select.astype(single_float)
    picker_low = select.astype(brain_half_float)
    argument_tuple = encoder_rows.astype(single_float)
    proj = jnp.einsum(
        "td,kde->kte", encoder_rows, triple_projection_matrix, preferred_element_type=single_float
    )
    shape_four = (nblock, block, local_heads, HEAD)
    queries_b = (proj[0] + asker_content_shifts[0]).astype(brain_half_float).reshape(shape_four)
    keys_b = proj[1].astype(brain_half_float).reshape(shape_four)
    values_b = (proj[2] + asker_content_shifts[1]).astype(brain_half_float).reshape(shape_four)
    scores = (
        jnp.einsum("bqhe,bkhe->bhqk", queries_b, keys_b, preferred_element_type=single_float)
        * scale
    )
    scores = jnp.where(same_seg, scores, masked_score)
    row_top = jnp.max(scores, axis=-1, keepdims=True)
    expo = jnp.exp(scores - row_top)
    row_total = jnp.sum(expo, axis=-1, keepdims=True)
    kept_lse = row_top + jnp.log(row_total)
    probs_b = (expo / row_total).astype(brain_half_float)
    mixed_b = (
        jnp.einsum("bhqk,bkhe->bqhe", probs_b, values_b, preferred_element_type=single_float)
        .reshape(rows, local_feat)
        .astype(brain_half_float)
    )
    attn_part = jnp.dot(mixed_b, mixing_result_matrix, preferred_element_type=single_float)
    resid_a = argument_tuple + row_sums(attn_part) + mixing_result_offset_vector
    hidden_a, norm_a_back = jax.vjp(
        layer_norm, resid_a, mixing_normalizer_scale, mixing_normalizer_shift
    )
    hidden_a_low = hidden_a.astype(brain_half_float)
    upper = (
        jnp.dot(hidden_a_low, widen_matrix, preferred_element_type=single_float)
        + widen_shift_vector
    )
    active, gelu_back = jax.vjp(exact_gelu, upper)
    active_b = active.astype(brain_half_float)
    ffn_part = jnp.dot(active_b, narrow_matrix, preferred_element_type=single_float)
    resid_b = hidden_a + row_sums(ffn_part) + narrow_shift_vector
    hidden_b, norm_b_back = jax.vjp(
        layer_norm, resid_b, perceptron_normalizer_scale, perceptron_normalizer_shift
    )
    hidden_b_low = hidden_b.astype(brain_half_float)
    query_vecs = jnp.dot(picker_low, hidden_b_low, preferred_element_type=single_float).astype(
        brain_half_float
    )
    unscaled_scores = lax.dot_general(
        lax.all_gather(query_vecs, "dp", axis=0, tiled=True),
        document_vectors,
        (((1,), (1,)), ((), ())),
        preferred_element_type=single_float,
    )
    sharpness_scalar = sharpness_factor[0]
    similarity_scores = unscaled_scores / sharpness_scalar
    offset = lax.axis_index(("dp", "mp")) * document_vectors.shape[0]
    local_ids = offset + jnp.arange(document_vectors.shape[0], dtype=jnp.int32)
    match_mask = correct_document_position[:, None] == local_ids[None, :]
    gold_part = jnp.sum(jnp.where(match_mask, similarity_scores, 0.0), axis=1)
    top = lax.pmax(jnp.max(similarity_scores, axis=1), ("dp", "mp"))
    weights = jnp.exp(similarity_scores - top[:, None])
    objective_accumulated, stability_shifter, correct_document_score = lax.psum(
        (jnp.sum(weights, axis=1), jnp.sum(weights * similarity_scores, axis=1), gold_part),
        ("dp", "mp"),
    )
    log_partition = top + jnp.log(objective_accumulated)
    seg_loss = log_partition - correct_document_score
    sharpness_derivative = jnp.reshape(
        -jnp.sum(stability_shifter / objective_accumulated - correct_document_score)
        / sharpness_scalar,
        (1,),
    )
    unscaled_score_grad = (
        (jnp.exp(similarity_scores - log_partition[:, None]) - match_mask.astype(single_float))
        / sharpness_scalar
    ).astype(brain_half_float)
    shares = lax.psum_scatter(
        jnp.dot(unscaled_score_grad, document_vectors, preferred_element_type=single_float),
        ("dp", "mp"),
        scatter_dimension=0,
        tiled=True,
    )
    d_query_vecs = lax.all_gather(shares, "mp", axis=0, tiled=True)
    d_hidden_b = upstream_sensitivity + jnp.dot(picker.T, d_query_vecs, precision=highest)
    d_resid_b, grad_second_gain, grad_second_shift = norm_b_back(d_hidden_b)
    grad_down_bias = jnp.sum(d_resid_b, axis=0)
    d_ffn_low = d_resid_b.astype(brain_half_float)
    grad_down_weight = lax.dot_general(
        active_b, d_ffn_low, (((0,), (0,)), ((), ())), preferred_element_type=single_float
    )
    d_active = lax.dot_general(
        d_ffn_low, narrow_matrix, (((1,), (1,)), ((), ())), preferred_element_type=single_float
    )
    d_upper_b = gelu_back(d_active)[0].astype(brain_half_float)
    grad_up_bias = jnp.sum(d_upper_b.astype(single_float), axis=0)
    grad_up_weight = lax.dot_general(
        hidden_a_low, d_upper_b, (((0,), (0,)), ((), ())), preferred_element_type=single_float
    )
    d_hidden_part = lax.dot_general(
        d_upper_b, widen_matrix, (((1,), (1,)), ((), ())), preferred_element_type=single_float
    )
    d_hidden_a = d_resid_b + row_sums(d_hidden_part)
    d_resid_a, grad_first_gain, grad_first_shift = norm_a_back(d_hidden_a)
    grad_out_bias = jnp.sum(d_resid_a, axis=0)
    d_attn_low = d_resid_a.astype(brain_half_float)
    grad_out_weight = lax.dot_general(
        mixed_b, d_attn_low, (((0,), (0,)), ((), ())), preferred_element_type=single_float
    )
    d_mixed_b = (
        lax.dot_general(
            d_attn_low,
            mixing_result_matrix,
            (((1,), (1,)), ((), ())),
            preferred_element_type=single_float,
        )
        .astype(brain_half_float)
        .reshape(shape_four)
    )
    again = (
        jnp.einsum("bqhe,bkhe->bhqk", queries_b, keys_b, preferred_element_type=single_float)
        * scale
    )
    again = jnp.where(same_seg, again, masked_score)
    probs = jnp.exp(again - kept_lse)
    probs_low = probs.astype(brain_half_float)
    d_values = jnp.einsum(
        "bhqk,bqhe->bkhe", probs_low, d_mixed_b, preferred_element_type=single_float
    )
    d_probs = jnp.einsum(
        "bqhe,bkhe->bhqk", d_mixed_b, values_b, preferred_element_type=single_float
    )
    d_scores_b = (
        probs * (d_probs - jnp.sum(d_probs * probs, axis=-1, keepdims=True)) * scale
    ).astype(brain_half_float)
    d_queries = jnp.einsum(
        "bhqk,bkhe->bqhe", d_scores_b, keys_b, preferred_element_type=single_float
    )
    d_keys = jnp.einsum(
        "bhqk,bqhe->bkhe", d_scores_b, queries_b, preferred_element_type=single_float
    )
    d_proj = jnp.stack(
        [
            d_queries.reshape(rows, local_feat),
            d_keys.reshape(rows, local_feat),
            d_values.reshape(rows, local_feat),
        ]
    ).astype(brain_half_float)
    d_proj_f = d_proj.astype(single_float)
    grad_head_bias = jnp.stack([jnp.sum(d_proj_f[0], axis=0), jnp.sum(d_proj_f[2], axis=0)])
    grad_head_weight = jnp.einsum(
        "td,kte->kde", encoder_rows, d_proj, preferred_element_type=single_float
    )
    d_input_part = jnp.einsum(
        "kte,kde->td", d_proj, triple_projection_matrix, preferred_element_type=single_float
    )
    grad_tokens = d_resid_a + row_sums(d_input_part)
    summed = lax.psum(
        (
            grad_head_weight,
            grad_head_bias,
            grad_out_weight,
            grad_out_bias,
            grad_first_gain,
            grad_first_shift,
            grad_up_weight,
            grad_up_bias,
            grad_down_weight,
            grad_down_bias,
            grad_second_gain,
            grad_second_shift,
        ),
        "dp",
    )
    return (
        hidden_b_low,
        seg_loss,
        grad_tokens,
        summed[0],
        summed[1],
        summed[2],
        summed[3],
        summed[4],
        summed[5],
        summed[6],
        summed[7],
        summed[8],
        summed[9],
        summed[10],
        summed[11],
        sharpness_derivative,
    )


def solution(mesh):
    in_specs = (
        P("dp", None),
        P("dp", None),
        P(None, None, "mp"),
        P(None, "mp"),
        P("mp", None),
        P(),
        P(),
        P(),
        P(None, "mp"),
        P("mp"),
        P("mp", None),
        P(),
        P(),
        P(),
        P(("dp", "mp"), None),
        P(),
        P(),
        P("dp", None),
    )
    out_specs = (
        P("dp", None),
        P(),
        P("dp", None),
        P(None, None, "mp"),
        P(None, "mp"),
        P("mp", None),
        P(),
        P(),
        P(),
        P(None, "mp"),
        P("mp"),
        P("mp", None),
        P(),
        P(),
        P(),
        P(),
    )
    return jax.shard_map(local, mesh=mesh, in_specs=in_specs, out_specs=out_specs, check_vma=False)
```

profile of v0, /device:TPU:0, one launch (start us, length us, event | category | flops | bytes accessed | tf_op | source)
XLA Modules:
  0.0 1185.5 jit_solution(8266141354047175256)
XLA Ops:
  7.2 4.3 convolution_bitcast_fusion.1
  12.5 2.0 fusion.112
  15.8 2.7 convert_element_type.80
  18.5 3.4 squeeze.12
  21.9 3.1 squeeze.13
  25.0 7.9 fusion.3
  33.0 7.5 fusion.2
  40.5 7.3 fusion.74
  49.5 3.7 fusion.114
  53.3 122.4 %all-reduce.9.cloned.1.call-done = f32[2048,768]{1,0:T(8,128)} async-done(((f32[2048,768]{1,0:T(8,128)}), f32[2048,768]{1,0:T(8,128)}) %all-reduce.9.cloned.1.call-update) | async-done | bytes 6291472 | tf_op jit(solution)/shard_map/psum | solution.py:25
  175.7 4.6 fusion.111
  183.0 18.3 %multiply_convert_fusion.1 = (bf16[2048,768]{1,0:T(8,128)(2,1)S(1)}, f32[2048,768]{1,0:T(8,128)}, f32[2048,768]{1,0:T(8,128)}) fusion(f32[768]{0:T(1024)S(1)} %copy-done.39, bf16[2048,768]{1,0:T(8,128)(2,1)S(1)} %fusion.39, bf16[768,768]{1,0:T(8,128)(2,1)S(1)} %copy-done), kind=kOutput, calls=%fused_computation.28 | convolution fusion | flops 2519728128 | bytes 20057088 | tf_op jit(solution)/shard_map/dot_general | solution.py:96
  203.0 4.5 fusion.115
  208.4 119.1 %all-reduce.11.cloned.1.call-done = f32[2048,768]{1,0:T(8,128)} async-done(((f32[2048,768]{1,0:T(8,128)}), f32[2048,768]{1,0:T(8,128)}) %all-reduce.11.cloned.1.call-update) | async-done | bytes 6291472 | tf_op jit(solution)/shard_map/psum | solution.py:25
  327.5 5.7 fusion.109
  338.0 31.3 %all_gather.6 = bf16[256,768]{1,0:T(8,128)(2,1)S(1)} all-gather(bf16[32,768]{1,0:T(8,128)(2,1)S(1)} %convolution_convert_fusion.1), channel_id=1, replica_groups=mesh['dp'=8,'mp'=4] {'dp'}, dimensions={0}, use_global_device_ids=true | all-gather | bytes 442368 | tf_op jit(solution)/shard_map/all_gather | solution.py:111
  369.4 3.8 fusion.113
  373.2 39.1 %pmax.7 = f32[256]{0:T(256)S(1)} all-reduce(f32[256]{0:T(256)S(1)} %get-tuple-element.66), channel_id=1, replica_groups=mesh['dp'=8,'mp'=4] {'dp','mp'}, use_global_device_ids=true, to_apply=%region_11.12 | all-reduce | flops 256 | bytes 2048 | tf_op jit(solution)/shard_map/pmax | solution.py:122
  412.3 3.2 multiply_reduce_fusion.7
  415.4 41.3 %all-reduce = (f32[256]{0:T(256)S(1)}, f32[256]{0:T(256)S(1)}, f32[256]{0:T(256)S(1)}) all-reduce(f32[256]{0:T(256)S(1)} %get-tuple-element.25, f32[256]{0:T(256)S(1)} %get-tuple-element.26, f32[256]{0:T(256)S(1)} %get-tuple-element.24), channel_id=1, replica_groups=mesh['dp'=8,'mp'=4] {'dp','mp'}, use_global_device_ids=true, to_apply=%region_13.14 | all-reduce | flops 768 | bytes 6144 | tf_op jit(solution)/shard_map/psum | solution.py:124
  457.9 7.2 fusion.48
  465.2 96.4 %reduce-scatter.2.cloned.1.call-done = f32[8,768]{1,0:T(8,128)} async-done(((f32[256,768]{1,0:T(8,128)}), f32[8,768]{1,0:T(8,128)}) %reduce-scatter.2.cloned.1.call-update) | async-done | bytes 24592 | tf_op jit(solution)/shard_map/reduce_scatter | solution.py:139
  561.6 5.5 all_gather.7
  567.1 8.7 multiply_reduce_fusion.1
  575.8 2.9 fusion.107
  578.7 10.3 convert_reduce_fusion
  590.6 4.5 fusion.116
  595.2 118.7 %all-reduce.13.cloned.1.call-done = f32[2048,768]{1,0:T(8,128)} async-done(((f32[2048,768]{1,0:T(8,128)}), f32[2048,768]{1,0:T(8,128)}) %all-reduce.13.cloned.1.call-update) | async-done | bytes 6291472 | tf_op jit(solution)/shard_map/psum | solution.py:25
  714.0 8.9 multiply_reduce_fusion.2
  722.9 4.3 fusion.106
  727.2 2.7 copy-done.3
  731.8 8.0 fusion.76
  739.8 7.4 fusion.71
  747.2 21.4 %fusion.65 = bf16[4,512,3,64]{1,3,2,0:T(8,128)(2,1)} fusion(f32[4,3,512,512]{2,3,1,0:T(8,128)} %fusion.76, f32[4,3,512,512]{2,3,1,0:T(8,128)} %get-tuple-element.64, f32[4,3,512]{2,1,0:T(4,128)S(1)} %log_add_fusion, pred[4,512,512]{1,2,0:T(8,128)(4,1)S(1)} %copy-done.9, f32[4,512,3,64]{1,0,3,2:T(4,128)} %squeeze.13, f32[3,64]{1,0:T(4,128)S(1)} %copy-done.23), kind=kOutput, calls=%fused_computation.92 | convolution fusion | flops 438442496 | bytes 28599040 | tf_op jit(solution)/shard_map/bhqk,bqhe->bkhe/dot_general | solution.py:200
  768.6 25.0 %fusion.68 = bf16[4,512,3,64]{1,3,2,0:T(8,128)(2,1)} fusion(f32[4,3,512,512]{2,3,1,0:T(8,128)} %fusion.76, f32[4,3,512,512]{2,3,1,0:T(8,128)} %get-tuple-element.64, f32[4,3,512]{2,1,0:T(4,128)S(1)} %log_add_fusion, pred[4,512,512]{1,2,0:T(8,128)(4,1)S(1)} %copy-done.9, bf16[4,512,3,64]{1,0,3,2:T(4,128)(2,1)S(1)} %copy-done.12), kind=kOutput, calls=%fused_computation.93 | convolution fusion | flops 437656064 | bytes 27811840 | tf_op jit(solution)/shard_map/bhqk,bkhe->bqhe/dot_general | solution.py:197
  793.6 1.8 copy.71
  796.9 1.7 copy.66
  805.8 5.7 convolution_bitcast_fusion
  811.8 7.1 fusion.117
  818.9 7.1 fusion.103
  826.1 1.8 fusion.105
  827.9 3.2 fusion.52
  832.8 98.6 %all-reduce.15.cloned.1.call-done = f32[2048,768]{1,0:T(8,128)} async-done(((f32[2048,768]{1,0:T(8,128)}), f32[2048,768]{1,0:T(8,128)}) %all-reduce.15.cloned.1.call-update) | async-done | bytes 6291472 | tf_op jit(solution)/shard_map/psum | solution.py:25
  931.4 7.7 add_reduce_fusion
  939.1 39.9 %all-reduce.1 = (f32[2,192]{1,0:T(2,128)}, f32[768]{0:T(1024)}, f32[768]{0:T(1024)}, f32[768]{0:T(1024)}, f32[768]{0:T(1024)}, /*index=5*/f32[768]{0:T(1024)}, f32[768]{0:T(1024)}, f32[768]{0:T(1024)}) all-reduce(f32[2,192]{1,0:T(2,128)S(1)} %pad_maximum_fusion, ...), channel_id=1, replica_groups=mesh['dp'=8,'mp'=4] {'dp'}, use_global_device_ids=true, to_apply=%region_27.28 | all-reduce | flops 5760 | bytes 46080 | tf_op jit(solution)/shard_map/psum | solution.py:219
  979.0 190.3 %all-reduce.17.cloned.1.call-done = (f32[3,768,192]{1,2,0:T(8,128)}, f32[192,768]{1,0:T(8,128)}, f32[768,768]{1,0:T(8,128)}, f32[768,768]{1,0:T(8,128)}) async-done(((f32[3,768,192]{1,2,0:T(8,128)}, f32[192,768]{1,0:T(8,128)}, f32[768,768]{1,0:T(8,128)}, f32[768,768]{1,0:T(8,128)}), (f32[3,768,192]{1,2,0:T(8,128)}, f32[192,768]{1,0:T(8,128)}, f32[768,768]{1,0:T(8,128)}, ...) | async-done | bytes 7077904 | tf_op jit(solution)/shard_map/psum | solution.py:219
  1169.4 2.9 copy.110
  1172.3 1.9 copy.111
  (154 shorter events, 30.9 us)
Async XLA Ops:
  7.2 175.8 %copy-start = (bf16[768,768]{1,0:T(8,128)(2,1)S(1)}, bf16[768,768]{1,0:T(8,128)(2,1)}, u32[]{:S(2)}) copy-start(bf16[768,768]{1,0:T(8,128)(2,1)} %param.26) | copy-start | bytes 3538948
  7.2 168.5 %all-reduce.9.cloned.1.call-start = ((), (), s32[]{:S(2)}) async-start(), calls=%async_computation.1 | async-start | bytes 12582912 | tf_op jit(solution)/shard_map/psum | solution.py:25
  11.5 3.0 copy-start.35
  11.5 3.2 copy-start.30
  14.7 18.3 %copy-start.22 = (f32[3,64]{1,0:T(4,128)}, f32[3,64]{1,0:T(4,128)S(1)}, u32[]{:S(2)}) copy-start(f32[3,64]{1,0:T(4,128)S(1)} %add.172) | copy-start | bytes 2308
  15.8 24.7 %copy-start.8 = (pred[4,512,512]{1,2,0:T(8,128)(4,1)}, pred[4,512,512]{1,2,0:T(8,128)(4,1)S(1)}, u32[]{:S(2)}) copy-start(pred[4,512,512]{1,2,0:T(8,128)(4,1)S(1)} %broadcast_compare_fusion) | copy-start | bytes 3145732
  18.5 14.5 %copy-start.11 = (bf16[4,512,3,64]{1,0,3,2:T(4,128)(2,1)}, bf16[4,512,3,64]{1,0,3,2:T(4,128)(2,1)S(1)}, u32[]{:S(2)}) copy-start(bf16[4,512,3,64]{1,0,3,2:T(4,128)(2,1)S(1)} %convert_element_type.80) | copy-start | bytes 2359300
  33.0 7.5 copy-start.10
  40.5 9.0 copy-start.17
  49.5 126.2 %copy-start.33 = (f32[768]{0:T(1024)S(1)}, f32[768]{0:T(1024)}, u32[]{:S(2)}) copy-start(f32[768]{0:T(1024)} %param.23) | copy-start | bytes 9220
  53.2 274.2 %all-reduce.11.cloned.1.call-start = ((), (), s32[]{:S(2)}) async-start(), calls=%async_computation.2 | async-start | bytes 12582912 | tf_op jit(solution)/shard_map/psum | solution.py:25
  180.3 2.6 copy-start.1
  181.2 1.7 copy-start.39
  182.9 18.3 %copy-start.13 = (bf16[2048,768]{1,0:T(8,128)(2,1)}, bf16[2048,768]{1,0:T(8,128)(2,1)S(1)}, u32[]{:S(2)}) copy-start(bf16[2048,768]{1,0:T(8,128)(2,1)S(1)} %fusion.39) | copy-start | bytes 9437188
  182.9 20.0 %copy-start.37 = (bf16[768,768]{1,0:T(8,128)(2,1)S(1)}, bf16[768,768]{1,0:T(8,128)(2,1)}, u32[]{:S(2)}) copy-start(bf16[768,768]{1,0:T(8,128)(2,1)} %param.28) | copy-start | bytes 3538948
  201.3 1.7 copy-start.41
  207.5 120.0 %copy-start.34 = (f32[768]{0:T(1024)S(1)}, f32[768]{0:T(1024)}, u32[]{:S(2)}) copy-start(f32[768]{0:T(1024)} %param.29) | copy-start | bytes 9220
  207.5 354.1 %reduce-scatter.2.cloned.1.call-start = ((), (), s32[]{:S(2)}) async-start(), calls=%async_computation.3 | async-start | bytes 811008 | tf_op jit(solution)/shard_map/reduce_scatter | solution.py:139
  333.2 3.2 copy-start.2
  333.2 36.1 %slice-start.4 = ((s8[6291456]{0:T(1024)(128)(4,1)}), s8[4194304]{0:T(1024)(128)(4,1)S(1)}, s32[]{:S(2)}) async-start(s8[6291456]{0:T(1024)(128)(4,1)} %bitcast.79), calls=%async_computation.11 | async-start | bytes 8388608
  334.1 35.2 %slice-start.5 = ((s8[6291456]{0:T(1024)(128)(4,1)}), s8[2097152]{0:T(1024)(128)(4,1)S(1)}, s32[]{:S(2)}) async-start(s8[6291456]{0:T(1024)(128)(4,1)} %bitcast.79), calls=%async_computation.12 | async-start | bytes 4194304
  369.4 42.9 %copy-start.36 = (s32[256]{0:T(256)S(1)}, s32[256]{0:T(256)}, u32[]{:S(2)}) copy-start(s32[256]{0:T(256)} %param.34) | copy-start | bytes 3076
  465.1 110.7 %slice-start = ((s8[6291456]{0:T(1024)(128)(4,1)}), s8[2097152]{0:T(1024)(128)(4,1)S(1)}, s32[]{:S(2)}) async-start(s8[6291456]{0:T(1024)(128)(4,1)} %bitcast.70), calls=%async_computation.7 | async-start | bytes 4194304
  465.1 248.8 %all-reduce.13.cloned.1.call-start = ((), (), s32[]{:S(2)}) async-start(), calls=%async_computation.4 | async-start | bytes 12582912 | tf_op jit(solution)/shard_map/psum | solution.py:25
  567.1 8.7 slice-start.1
  575.8 2.9 copy-start.38
  578.7 10.3 copy-start.4
  595.2 336.3 %all-reduce.15.cloned.1.call-start = ((), (), s32[]{:S(2)}) async-start(), calls=%async_computation.5 | async-start | bytes 12582912 | tf_op jit(solution)/shard_map/psum | solution.py:25
  722.9 7.0 copy-start.18
  727.2 2.7 copy-start.3
  731.8 8.0 copy-start.9
  739.8 7.4 copy-start.23
  747.2 21.4 %copy-start.12 = (bf16[4,512,3,64]{1,0,3,2:T(4,128)(2,1)S(1)}, bf16[4,512,3,64]{1,0,3,2:T(4,128)(2,1)}, u32[]{:S(2)}) copy-start(bf16[4,512,3,64]{1,0,3,2:T(4,128)(2,1)} %copy-done.11) | copy-start | bytes 2359300
  793.6 6.5 copy-start.19
  811.5 357.9 %all-reduce.17.cloned.1.call-start = ((), (), s32[]{:S(2)}) async-start(), calls=%async_computation.6 | async-start | bytes 14155776 | tf_op jit(solution)/shard_map/psum | solution.py:219
  811.8 7.1 copy-start.42
  811.8 14.2 %slice-start.2 = ((s8[6291456]{0:T(1024)(128)(4,1)}), s8[4194304]{0:T(1024)(128)(4,1)S(1)}, s32[]{:S(2)}) async-start(s8[6291456]{0:T(1024)(128)(4,1)} %bitcast.72), calls=%async_computation.9 | async-start | bytes 8388608
  818.9 7.1 slice-start.3
  818.9 7.1 copy-start.7
  826.0 1.9 copy-start.14
  832.7 106.3 %copy-start.24 = (f32[768]{0:T(1024)S(1)}, f32[768]{0:T(1024)}, u32[]{:S(2)}) copy-start(f32[768]{0:T(1024)} %get-tuple-element.16) | copy-start | bytes 9220
  832.8 106.3 %copy-start.25 = (f32[768]{0:T(1024)S(1)}, f32[768]{0:T(1024)}, u32[]{:S(2)}) copy-start(f32[768]{0:T(1024)} %get-tuple-element.20) | copy-start | bytes 9220
  832.8 106.3 %copy-start.27 = (f32[768]{0:T(1024)S(1)}, f32[768]{0:T(1024)}, u32[]{:S(2)}) copy-start(f32[768]{0:T(1024)} %get-tuple-element.18) | copy-start | bytes 9220
  832.8 106.3 %copy-start.28 = (f32[768]{0:T(1024)S(1)}, f32[768]{0:T(1024)}, u32[]{:S(2)}) copy-start(f32[768]{0:T(1024)} %get-tuple-element.21) | copy-start | bytes 9220
  832.8 106.3 %copy-start.29 = (f32[768]{0:T(1024)S(1)}, f32[768]{0:T(1024)}, u32[]{:S(2)}) copy-start(f32[768]{0:T(1024)} %get-tuple-element.57) | copy-start | bytes 9220
  832.8 106.3 %copy-start.32 = (f32[768]{0:T(1024)S(1)}, f32[768]{0:T(1024)}, u32[]{:S(2)}) copy-start(f32[768]{0:T(1024)} %get-tuple-element.69) | copy-start | bytes 9220
  1169.3 4.9 copy-start.16
  1169.4 6.3 copy-start.15
  (7 other events, 7.9 us)
Sparse Core Ops, SparseCore 0:
  53.4 122.2 all-reduce.8
  207.6 119.7 all-reduce.10
  465.3 96.2 reduce-scatter.1
  595.3 118.6 all-reduce.12
  811.6 119.7 all-reduce.14
  936.8 232.4 all-reduce.16
where the time goes:
time: 1200 us; the launch traced here: 1190 us
  waiting for transfers between devices  746 us (62%)
  matrix products  169 us (14%)
  blocking collectives  157 us (13%)
  other arithmetic  51.8 us (4%)
  local copies, waits for them, and re-layouts  43.4 us (4%)
  between operations  17.8 us (1%)
    psum x4, waiting for transfers between devices, row_sums(): return lax.psum(part, 'mp')  459 us
    psum x1, waiting for transfers between devices, local(): lax.psum((grad_head_weight, grad_head_bias, grad_out_weight, grad_out_bia...  190 us
    reduce_scatter x1, waiting for transfers between devices, local(): lax.psum_scatter(jnp.dot(unscaled_score_grad, document_vectors, preferred...  96.4 us
    psum x1, blocking collectives, local(): lax.psum((jnp.sum(weights, axis=1), jnp.sum(weights * similarity_scores,...  41.3 us
    psum x1, blocking collectives, local(): lax.psum((grad_head_weight, grad_head_bias, grad_out_weight, grad_out_bia...  39.9 us
    pmax x1, blocking collectives, local(): top = lax.pmax(jnp.max(similarity_scores, axis=1), ('dp', 'mp'))  39.1 us
    all_gather x1, blocking collectives, local(): lax.all_gather(query_vecs, 'dp', axis=0, tiled=True)  31.3 us
    dot_general x1, matrix products, local(): jnp.einsum('bhqk,bkhe->bqhe', d_scores_b, keys_b, preferred_element_type=...  25 us
  transfers between devices with their start and end apart: 6, of which 6 were waited for; matrix products, arithmetic and copies ran while one was open for 2% of the time, Pallas kernels for 0%

commit v1 on v0

v1 whole, which is shorter than its diff:
```python
import functools

import jax
import jax.numpy as jnp
from jax import lax
from jax.experimental import pallas as pl
from jax.experimental.pallas import tpu as pltpu
from jax.sharding import PartitionSpec as P

HEAD = 64
F32 = jnp.float32
BF16 = jnp.bfloat16
MESH = pl.DeviceIdType.MESH
norm_epsilon = 1e-05
masked_score = -1e30


def dot(a, b, ca, cb):
    return lax.dot_general(a, b, (((ca,), (cb,)), ((), ())), preferred_element_type=F32)


def norm_stats(resid):
    centre = jnp.mean(resid, axis=-1, keepdims=True)
    centred = resid - centre
    spread = jnp.mean(centred * centred, axis=-1, keepdims=True)
    inv = lax.rsqrt(spread + norm_epsilon)
    return centred * inv, inv


def norm_back(d_out, normed, inv, gain):
    e = d_out * gain
    return inv * (
        e - jnp.mean(e, axis=-1, keepdims=True) - normed * jnp.mean(e * normed, axis=-1, keepdims=True)
    )


def swap(value, width, distance):
    return lax.ppermute(value, "mp", [(i, i ^ distance) for i in range(width)])


def spread_over_mp(own, width):
    held = [own]
    order = [0]
    step = width // 2
    while step:
        held = held + [swap(h, width, step) for h in held]
        order = order + [o ^ step for o in order]
        step //= 2
    return [held[order.index(r)] for r in range(width)]


def gather_back(parts, width):
    parts = list(parts)
    step = 1
    while step < width:
        new = {}
        for r in range(width):
            if not (r & (step - 1)) and not (r & step):
                got = swap(parts[r | step].astype(BF16), width, step)
                new[r] = parts[r] + got.astype(F32)
        for r, v in new.items():
            parts[r] = v
        step *= 2
    return parts[0]


def retrieval_kernel(
    ndp, nmp, query_ref, docs_hbm, gold_ref, sharp_ref, dq_ref, loss_ref, ds_ref,
    queries, docs, low, stats, columns, part_u, part_g, send, got, doc_sem, q_send, q_recv, s_send, s_recv, d_send, d_recv,
):
    n = ndp * nmp
    own = query_ref.shape[0]
    nseg = gold_ref.shape[0]
    tile = 256 if nseg <= 256 else 128
    dp, mp = lax.axis_index("dp"), lax.axis_index("mp")
    me = dp * nmp + mp
    load = pltpu.make_async_copy(docs_hbm, docs, doc_sem)
    load.start()
    barrier = pltpu.get_barrier_semaphore()

    def device(step):
        other = lax.rem(me + step, n)
        return other, (other // nmp, lax.rem(other, nmp))

    @pl.loop(1, n)
    def _(step):
        _, where = device(step)
        pl.semaphore_signal(barrier, inc=1, device_id=where, device_id_type=MESH)

    pl.semaphore_wait(barrier, n - 1)

    def push(source, target, send_sems, recv_sems):
        @pl.loop(1, n)
        def _(step):
            other, where = device(step)
            pltpu.make_async_remote_copy(
                source(other), target, send_sems.at[step], recv_sems.at[step], device_id=where, device_id_type=MESH
            ).start()

    def drain(source, target, send_sems, recv_sems):
        @pl.loop(1, n)
        def _(step):
            other, where = device(step)
            copy = pltpu.make_async_remote_copy(
                source(other), target, send_sems.at[step], recv_sems.at[step], device_id=where, device_id_type=MESH
            )
            copy.wait()

    push(lambda other: query_ref, queries.at[me], q_send, q_recv)
    queries[me] = query_ref[...]
    drain(lambda other: query_ref, queries.at[me], q_send, q_recv)
    load.wait()

    sharp = sharp_ref[0]
    offset = me * docs.shape[0]
    ids = lax.broadcasted_iota(jnp.int32, (tile, docs.shape[0]), 1)
    lane = lax.broadcasted_iota(jnp.int32, (tile, 128), 1)
    per = tile // own

    @pl.loop(0, nseg // tile)
    def _(i):
        span = pl.ds(pl.multiple_of(i * tile, tile), tile)
        q = queries[pl.ds(i * per, per)].reshape(tile, queries.shape[2])
        logit = lax.dot_general(q, docs[...], (((1,), (1,)), ((), ())), preferred_element_type=F32) / sharp
        match = ids == gold_ref[span, :] - offset
        top = jnp.max(logit, axis=1, keepdims=True)
        expo = jnp.exp(logit - top)
        total = jnp.sum(expo, axis=1, keepdims=True)
        tilt = jnp.sum(expo * logit, axis=1, keepdims=True)
        gold = jnp.sum(jnp.where(match, logit, 0.0), axis=1, keepdims=True)
        packed = jnp.where(lane == 0, top, jnp.where(lane == 1, total, jnp.where(lane == 2, tilt, gold)))
        stats[me, :, span] = packed.T[:4]
        low[span, :] = jnp.where(match, 0.0, expo).astype(BF16)

    push(lambda other: stats.at[me], stats.at[me], s_send, s_recv)

    @pl.loop(0, nseg // tile)
    def _(i):
        span = pl.ds(pl.multiple_of(i * tile, tile), tile)
        part_u[span, :] = jnp.dot(low[span, :], docs[...], preferred_element_type=F32)
        match = ids == gold_ref[span, :] - offset
        part_g[span, :] = jnp.dot(
            match.astype(F32).astype(BF16), docs[...], preferred_element_type=F32
        ).astype(BF16)

    drain(lambda other: stats.at[me], stats.at[me], s_send, s_recv)

    tops = stats[:, 0, :]
    top = jnp.max(tops, axis=0, keepdims=True)
    share = jnp.exp(tops - top)
    total = jnp.sum(stats[:, 1, :] * share, axis=0, keepdims=True)
    tilt = jnp.sum(stats[:, 2, :] * share, axis=0, keepdims=True)
    gold = jnp.sum(stats[:, 3, :], axis=0, keepdims=True)
    lse = top + jnp.log(total)
    loss_ref[...] = lse - gold
    ds_ref[...] = -jnp.sum(tilt / total - gold, axis=1, keepdims=True) / sharp
    scale = jnp.exp(stats[me, 0:1, :] - lse) / sharp
    gold_scale = (jnp.exp(gold - lse) - 1.0) / sharp
    row = lax.broadcasted_iota(jnp.int32, (128, nseg), 0)
    columns[...] = jnp.where(row == 0, scale, gold_scale).T

    @pl.loop(0, nseg // tile)
    def _(i):
        span = pl.ds(pl.multiple_of(i * tile, tile), tile)
        value = part_u[span, :] * columns[span, 0:1] + part_g[span, :].astype(F32) * columns[span, 1:2]
        send[pl.ds(i * per, per)] = value.astype(BF16).reshape(per, own, value.shape[1])

    push(lambda other: send.at[other], got.at[me], d_send, d_recv)
    got[me] = send[me]
    drain(lambda other: send.at[other], got.at[me], d_send, d_recv)
    dq_ref[...] = jnp.sum(got[...].astype(F32), axis=0)


def retrieval(query, docs, gold, sharp, ndp, nmp):
    n = ndp * nmp
    own, width = query.shape
    nseg = gold.shape[0]
    vmem = pl.BlockSpec(memory_space=pltpu.VMEM)
    return pl.pallas_call(
        functools.partial(retrieval_kernel, ndp, nmp),
        out_shape=(
            jax.ShapeDtypeStruct((own, width), F32),
            jax.ShapeDtypeStruct((1, nseg), F32),
            jax.ShapeDtypeStruct((1, 1), F32),
        ),
        in_specs=[vmem, pl.BlockSpec(memory_space=pl.ANY), vmem, pl.BlockSpec(memory_space=pltpu.SMEM)],
        out_specs=(vmem, vmem, vmem),
        scratch_shapes=[
            pltpu.VMEM((n, own, width), BF16),
            pltpu.VMEM(docs.shape, BF16),
            pltpu.VMEM((nseg, docs.shape[0]), BF16),
            pltpu.VMEM((n, 4, nseg), F32),
            pltpu.VMEM((nseg, 128), F32),
            pltpu.VMEM((nseg, width), F32),
            pltpu.VMEM((nseg, width), BF16),
            pltpu.VMEM((n, own, width), BF16),
            pltpu.VMEM((n, own, width), BF16),
            pltpu.SemaphoreType.DMA,
        ]
        + [pltpu.SemaphoreType.DMA((n,))] * 6,
        compiler_params=pltpu.CompilerParams(
            collective_id=0, has_side_effects=True, vmem_limit_bytes=60 * 2**20
        ),
        name="retrieval",
    )(query, docs, gold, sharp)


def attention(q, k, v, same):
    rows, feat = q.shape
    heads = feat // HEAD
    shape = (rows, heads, HEAD)
    scores = jnp.einsum("qhe,khe->hqk", q.reshape(shape), k.reshape(shape), preferred_element_type=F32)
    scores = jnp.where(same[None], scores * HEAD ** (-0.5), masked_score)
    top = jnp.max(scores, axis=-1, keepdims=True)
    expo = jnp.exp(scores - top)
    total = jnp.sum(expo, axis=-1, keepdims=True)
    probs = (expo / total).astype(BF16)
    mixed = jnp.einsum("hqk,khe->qhe", probs, v.reshape(shape), preferred_element_type=F32)
    return mixed.reshape(rows, feat).astype(BF16), top + jnp.log(total)


def attention_back(q, k, v, lse, d_mixed, same):
    rows, feat = q.shape
    heads = feat // HEAD
    shape = (rows, heads, HEAD)
    scale = HEAD ** (-0.5)
    q, k, v, d_mixed = (t.reshape(shape) for t in (q, k, v, d_mixed))
    scores = jnp.einsum("qhe,khe->hqk", q, k, preferred_element_type=F32)
    scores = jnp.where(same[None], scores * scale, masked_score)
    probs = jnp.exp(scores - lse)
    d_v = jnp.einsum("hqk,qhe->khe", probs.astype(BF16), d_mixed, preferred_element_type=F32)
    d_p = jnp.einsum("qhe,khe->hqk", d_mixed, v, preferred_element_type=F32)
    d_s = (probs * (d_p - jnp.sum(d_p * probs, axis=-1, keepdims=True)) * scale).astype(BF16)
    d_q = jnp.einsum("hqk,khe->qhe", d_s, k, preferred_element_type=F32)
    d_k = jnp.einsum("hqk,qhe->khe", d_s, q, preferred_element_type=F32)
    return tuple(t.reshape(rows, feat).astype(BF16) for t in (d_q, d_k, d_v))


def local(
    encoder_rows,
    piece_extent_sequence,
    triple_projection_matrix,
    asker_content_shifts,
    mixing_result_matrix,
    mixing_result_offset_vector,
    mixing_normalizer_scale,
    mixing_normalizer_shift,
    widen_matrix,
    widen_shift_vector,
    narrow_matrix,
    narrow_shift_vector,
    perceptron_normalizer_scale,
    perceptron_normalizer_shift,
    document_vectors,
    sharpness_factor,
    correct_document_position,
    upstream_sensitivity,
    *,
    width,
    depth,
):
    everyone = ("dp", "mp")
    me = lax.axis_index("mp")
    nblock, nseg_block = piece_extent_sequence.shape
    block = encoder_rows.shape[0] // nblock
    own_blocks = nblock // width
    rows = own_blocks * block
    feat = triple_projection_matrix.shape[2]
    quarters = range(width)

    x = lax.dynamic_slice_in_dim(encoder_rows, me * rows, rows, 0)
    upstream = lax.dynamic_slice_in_dim(upstream_sensitivity, me * rows, rows, 0)
    extents = lax.dynamic_slice_in_dim(piece_extent_sequence, me * own_blocks, own_blocks, 0)

    w_qkv = spread_over_mp(triple_projection_matrix, width)
    small = spread_over_mp(
        jnp.concatenate([asker_content_shifts.reshape(-1), widen_shift_vector])[None], width
    )
    w_out = spread_over_mp(mixing_result_matrix, width)
    w_up = spread_over_mp(widen_matrix, width)
    w_down = spread_over_mp(narrow_matrix, width)
    b_q = [s[:, :feat] for s in small]
    b_v = [s[:, feat : 2 * feat] for s in small]
    b_up = [s[:, 2 * feat :] for s in small]

    ends = jnp.cumsum(extents, axis=1)
    starts = ends - extents
    places = jnp.arange(rows, dtype=jnp.int32)
    base = (jnp.arange(own_blocks, dtype=jnp.int32) * block)[:, None]
    seg = jnp.sum((places[:, None] >= (ends + base).reshape(-1)[None]).astype(jnp.int32), axis=1)
    same = seg[:, None] == seg[None, :]
    firsts = (starts + base).reshape(-1)
    select = firsts[:, None] == places[None, :]
    pick = select.astype(BF16)

    qs, ks, vs, lses, mixed = [], [], [], [], []
    for r in quarters:
        proj = jnp.einsum("td,kde->kte", x, w_qkv[r], preferred_element_type=F32)
        q = (proj[0] + b_q[r]).astype(BF16)
        k = proj[1].astype(BF16)
        v = (proj[2] + b_v[r]).astype(BF16)
        m, lse = attention(q, k, v, same)
        qs.append(q), ks.append(k), vs.append(v), lses.append(lse), mixed.append(m)
    attn_out = sum(dot(mixed[r], w_out[r], 1, 0) for r in quarters)
    n1, inv1 = norm_stats(x.astype(F32) + attn_out + mixing_result_offset_vector)
    h1 = n1 * mixing_normalizer_scale + mixing_normalizer_shift
    h1_low = h1.astype(BF16)
    acts, slopes = [], []
    for r in quarters:
        upper = dot(h1_low, w_up[r], 1, 0) + b_up[r]
        act, back = jax.vjp(lambda u: jax.nn.gelu(u, approximate=False), upper)
        acts.append(act.astype(BF16))
        slopes.append(back(jnp.ones_like(upper))[0])
    ffn_out = sum(dot(acts[r], w_down[r], 1, 0) for r in quarters)
    n2, inv2 = norm_stats(h1 + ffn_out + narrow_shift_vector)
    h2 = n2 * perceptron_normalizer_scale + perceptron_normalizer_shift
    own_out = h2.astype(BF16)
    layer_out = lax.all_gather(own_out, "mp", axis=0, tiled=True)

    query = dot(pick, own_out, 1, 0).astype(BF16)
    d_query, seg_loss, sharpness_derivative = retrieval(
        query, document_vectors, correct_document_position[:, None], sharpness_factor, depth, width
    )
    seg_loss = seg_loss[0]
    sharpness_derivative = sharpness_derivative[0]
    d_h2 = upstream + lax.dot_general(
        select.astype(F32), d_query, (((0,), (0,)), ((), ())), precision=lax.Precision.HIGHEST
    )
    d_r2 = norm_back(d_h2, n2, inv2, perceptron_normalizer_scale)
    g_second_gain = jnp.sum(d_h2 * n2, axis=0)
    g_second_shift = jnp.sum(d_h2, axis=0)
    g_down_bias = jnp.sum(d_r2, axis=0)
    d_ffn = d_r2.astype(BF16)
    g_down = gather_back([dot(acts[r], d_ffn, 0, 0) for r in quarters], width)
    d_up = [(dot(d_ffn, w_down[r], 1, 1) * slopes[r]).astype(BF16) for r in quarters]
    g_up_bias = [jnp.sum(d.astype(F32), axis=0) for d in d_up]
    g_up = gather_back([dot(h1_low, d_up[r], 0, 0) for r in quarters], width)
    d_h1 = d_r2 + sum(dot(d_up[r], w_up[r], 1, 1) for r in quarters)
    d_r1 = norm_back(d_h1, n1, inv1, mixing_normalizer_scale)
    g_first_gain = jnp.sum(d_h1 * n1, axis=0)
    g_first_shift = jnp.sum(d_h1, axis=0)
    g_out_bias = jnp.sum(d_r1, axis=0)
    d_attn = d_r1.astype(BF16)
    g_out = gather_back([dot(mixed[r], d_attn, 0, 0) for r in quarters], width)
    d_tokens = d_r1
    g_qkv, g_head_bias = [], []
    for r in quarters:
        d_mixed = dot(d_attn, w_out[r], 1, 1).astype(BF16)
        d_q, d_k, d_v = attention_back(qs[r], ks[r], vs[r], lses[r], d_mixed, same)
        d_proj = (d_q, d_k, d_v)
        g_qkv.append(jnp.stack([dot(x, d, 0, 0) for d in d_proj]))
        g_head_bias.append(
            jnp.concatenate([jnp.sum(d_q.astype(F32), axis=0), jnp.sum(d_v.astype(F32), axis=0)])
        )
        d_tokens = d_tokens + sum(dot(d_proj[k], w_qkv[r][k], 1, 1) for k in range(3))
    g_qkv = gather_back(g_qkv, width)
    grad_tokens = lax.all_gather(d_tokens.astype(BF16), "mp", axis=0, tiled=True).astype(F32)

    def over_dp(part):
        return lax.psum(part.astype(BF16), "dp").astype(F32)

    whole = jnp.stack(
        [g_out_bias, g_first_gain, g_first_shift, g_down_bias, g_second_gain, g_second_shift]
    )
    split = jnp.zeros((width, 1, 2 * feat + g_up_bias[0].shape[0]), F32)
    for r in quarters:
        split = lax.dynamic_update_slice(
            split, jnp.concatenate([g_head_bias[r], g_up_bias[r]])[None, None], (me ^ r, 0, 0)
        )
    whole, split = lax.psum((whole, split), everyone)
    mine = lax.dynamic_slice_in_dim(split, me, 1, 0)[0, 0]
    return (
        layer_out,
        seg_loss,
        grad_tokens,
        over_dp(g_qkv),
        mine[: 2 * feat].reshape(2, feat),
        over_dp(g_out),
        whole[0],
        whole[1],
        whole[2],
        over_dp(g_up),
        mine[2 * feat :],
        over_dp(g_down),
        whole[3],
        whole[4],
        whole[5],
        sharpness_derivative,
    )


def solution(mesh):
    in_specs = (
        P("dp", None),
        P("dp", None),
        P(None, None, "mp"),
        P(None, "mp"),
        P("mp", None),
        P(),
        P(),
        P(),
        P(None, "mp"),
        P("mp"),
        P("mp", None),
        P(),
        P(),
        P(),
        P(("dp", "mp"), None),
        P(),
        P(),
        P("dp", None),
    )
    out_specs = (
        P("dp", None),
        P(),
        P("dp", None),
        P(None, None, "mp"),
        P(None, "mp"),
        P("mp", None),
        P(),
        P(),
        P(),
        P(None, "mp"),
        P("mp"),
        P("mp", None),
        P(),
        P(),
        P(),
        P(),
    )
    width = mesh.shape["mp"]

    def step(*args):
        return local(*args, width=width, depth=mesh.shape["dp"])

    return jax.shard_map(step, mesh=mesh, in_specs=in_specs, out_specs=out_specs, check_vma=False)
```

time: 1200 us -> 585 us (0.49)
  waiting for transfers between devices: 746 us -> 219 us
  blocking collectives: 157 us -> 46.4 us
  Pallas kernels: 0 us -> 37.2 us
  other arithmetic: 51.8 us -> 28.4 us
  local copies, waits for them, and re-layouts: 43.4 us -> 22 us
  starting transfers between devices: 0.54 us -> 17 us
  matrix products: 169 us -> 185 us
    psum x5 -> x1, waiting for transfers between devices: 649 us -> 86.9 us  [over_dp(): return lax.psum(part.astype(BF16), 'dp').astype(F32)]
    ppermute x0 -> x27, waiting for transfers between devices: none -> 132 us  [swap(): return lax.ppermute(value, 'mp', [(i, i ^ distance) for i in range(width)])]
    reduce_scatter x1 -> x0, waiting for transfers between devices: 96.4 us -> none  [local(): lax.psum_scatter(jnp.dot(unscaled_score_grad, document_vectors, preferred...]
    reduce_sum x12 -> x9, other arithmetic: 46.6 us -> 4.65 us  [the longest x4 1.77 us: attention(): total = jnp.sum(expo, axis=-1, keepdims=True)]
    pmax x1 -> x0, blocking collectives: 39.1 us -> none  [local(): top = lax.pmax(jnp.max(similarity_scores, axis=1), ('dp', 'mp'))]
    pallas_call x0 -> x1, Pallas kernels: none -> 37.2 us  [retrieval(): pl.pallas_call(functools.partial(retrieval_kernel, ndp, nmp), out_shape=(...]
    all_gather x2 -> x0, blocking collectives: 36.8 us -> none  [the longest x1 31.3 us: local(): lax.all_gather(query_vecs, 'dp', axis=0, tiled=True)]
    psum x2 -> x1, blocking collectives: 81.2 us -> 46.4 us  [local(): whole, split = lax.psum((whole, split), everyone)]
  transfers between devices with their start and end apart: 6 -> 30, of which waited for: 6 -> 7; matrix products, arithmetic and copies ran while one was open for 2% -> 16% of each run, Pallas kernels for 0% -> 0%
where the time goes in v1:
time: 585 us; the launch traced here: 575 us
  waiting for transfers between devices  219 us (37%)
  matrix products  185 us (32%)
  blocking collectives  46.4 us (8%)
  Pallas kernels  37.2 us (6%)
  other arithmetic  28.4 us (5%)
  local copies, waits for them, and re-layouts  22 us (4%)
  between operations  20.3 us (3%)
  starting transfers between devices  17 us (3%)
    ppermute x27, waiting for transfers between devices, swap(): return lax.ppermute(value, 'mp', [(i, i ^ distance) for i in range(width)])  132 us
    dot_general x61, matrix products, dot(): lax.dot_general(a, b, (((ca,), (cb,)), ((), ())), preferred_element_type=...  87.6 us
    psum x1, waiting for transfers between devices, over_dp(): return lax.psum(part.astype(BF16), 'dp').astype(F32)  86.9 us
    psum x1, blocking collectives, local(): whole, split = lax.psum((whole, split), everyone)  46.4 us
    pallas_call x1, Pallas kernels, retrieval(): pl.pallas_call(functools.partial(retrieval_kernel, ndp, nmp), out_shape=(...  37.2 us
    dot_general x4, matrix products, attention_back(): d_q = jnp.einsum('hqk,khe->qhe', d_s, k, preferred_element_type=F32)  30.1 us
    dot_general x4, matrix products, attention_back(): d_k = jnp.einsum('hqk,qhe->khe', d_s, q, preferred_element_type=F32)  28.8 us
    ppermute x27, starting transfers between devices, swap(): return lax.ppermute(value, 'mp', [(i, i ^ distance) for i in range(width)])  16.6 us
  transfers between devices with their start and end apart: 30, of which 7 were waited for; matrix products, arithmetic and copies ran while one was open for 16% of the time, Pallas kernels for 0%

profile of v1, /device:TPU:0, one launch (start us, length us, event | category | flops | bytes accessed | tf_op | source)
XLA Modules:
  0.0 575.2 jit_solution(12463639116027610239)
XLA Ops:
  8.6 2.6 collective-permute-start.3
  13.2 2.1 fusion.206
  23.4 1.8 collective-permute-start.5
  25.2 6.8 %collective-permute-done.4 = f32[1,1152]{1,0:T(1,128)S(1)} collective-permute-done((f32[1,1152]{1,0:T(1,128)S(1)}, f32[1,1152]{1,0:T(1,128)S(1)}, u32[]{:S(2)}, u32[]{:S(2)}) %collective-permute-start.4) | collective-permute-done | bytes 4640 | tf_op jit(solution)/shard_map/ppermute | solution.py:38
  33.2 2.0 collective-permute-start.11
  35.6 1.8 fusion.205
  37.5 2.1 fusion.204
  48.4 15.3 %collective-permute-done.11 = bf16[768,768]{1,0:T(8,128)(2,1)} collective-permute-done((bf16[768,768]{1,0:T(8,128)(2,1)}, bf16[768,768]{1,0:T(8,128)(2,1)}, u32[]{:S(2)}, u32[]{:S(2)}) %collective-permute-start.11) | collective-permute-done | bytes 1179680 | tf_op jit(solution)/shard_map/ppermute | solution.py:38
  63.7 24.9 %collective-permute-done.12 = bf16[768,768]{1,0:T(8,128)(2,1)S(1)} collective-permute-done((bf16[768,768]{1,0:T(8,128)(2,1)}, bf16[768,768]{1,0:T(8,128)(2,1)S(1)}, u32[]{:S(2)}, u32[]{:S(2)}) %collective-permute-start.12) | collective-permute-done | bytes 1179680 | tf_op jit(solution)/shard_map/ppermute | solution.py:38
  95.9 5.5 multiply_convert_fusion.11
  101.4 6.7 %multiply_convert_fusion.9 = (bf16[512,768]{1,0:T(8,128)(2,1)S(1)}, f32[512,768]{1,0:T(8,128)}, f32[512,768]{1,0:T(8,128)}) fusion(f32[768]{0:T(1024)S(1)} %slice_reduce_fusion.7, bf16[512,768]{1,0:T(8,128)(2,1)S(1)} %fusion.115, bf16[768,768]{1,0:T(8,128)(2,1)} %collective-permute-done.11), kind=kOutput, calls=%fused_computation.114 | convolution fusion | flops 629932032 | bytes 5901312 | tf_op jit(solution)/shard_map/dot_general | solution.py:19
  108.1 5.5 multiply_convert_fusion.10
  116.9 5.6 multiply_convert_fusion.8
  125.7 37.2 %retrieval.1 = (f32[8,768]{1,0:T(8,128)}, f32[1,256]{1,0:T(1,128)}, f32[1,1]{1,0:T(1,128)}) custom-call(bf16[8,768]{1,0:T(8,128)(2,1)} %convolution_convert_fusion.16.query_ref, bf16[4096,768]{1,0:T(8,128)(2,1)} %docs_hbm.1, s32[256,1]{1,0:T(8,128)} %copy.71.gold_ref, f32[1]{0:T(128)S(6)} %copy.111.sharp_ref), custom_call_target="tpu_custom_call" | custom-call | tf_op jit(solution)/shard_map/retrieval/pallas_call | solution.py:179
  162.9 3.5 multiply_reduce_fusion.4
  178.2 2.4 fusion.239
  182.4 2.0 multiply_reduce_fusion.5
  187.0 2.5 fusion.181
  189.5 7.1 %fusion.153 = bf16[3,64,512]{2,1,0:T(8,128)(2,1)} fusion(f32[3,512,512]{1,2,0:T(8,128)} %fusion.181, f32[3,512,512]{1,2,0:T(8,128)} %copy-done.7, f32[3,512]{1,0:T(4,128)} %log_add_fusion.2, f32[512,3,64]{0,2,1:T(8,128)} %bitcast.317, f32[3,64]{1,0:T(4,128)} %copy-done.100), kind=kOutput, calls=%fused_computation.218 | convolution fusion | flops 106465280 | bytes 6888192 | tf_op jit(solution)/shard_map/hqk,qhe->khe/dot_general | solution.py:235
  196.6 7.8 %convert_reduce_fusion.9 = (f32[3,64]{1,0:T(4,128)}, bf16[3,64,512]{2,1,0:T(8,128)(2,1)}) fusion(bf16[512,3,64]{0,2,1:T(8,128)(2,1)S(1)} %bitcast.329, f32[3,512,512]{1,2,0:T(8,128)} %fusion.181, f32[3,512,512]{1,2,0:T(8,128)} %copy-done.7, f32[3,512]{1,0:T(4,128)} %log_add_fusion.2), kind=kOutput, calls=%fused_computation.240 | convolution fusion | flops 106465088 | bytes 6691584 | tf_op jit(solution)/shard_map/hqk,khe->qhe/dot_general | solution.py:234
  204.4 3.8 convert_reduce_fusion.8
  208.7 2.4 fusion.183
  212.4 7.1 %fusion.141 = bf16[3,64,512]{2,1,0:T(8,128)(2,1)} fusion(f32[3,512,512]{1,2,0:T(8,128)} %fusion.183, f32[3,512,512]{1,2,0:T(8,128)} %copy-done.8, f32[3,512]{1,0:T(4,128)} %log_add_fusion, f32[512,3,64]{0,2,1:T(8,128)} %bitcast.321, f32[3,64]{1,0:T(4,128)} %copy-done.99), kind=kOutput, calls=%fused_computation.214 | convolution fusion | flops 106465280 | bytes 6888192 | tf_op jit(solution)/shard_map/hqk,qhe->khe/dot_general | solution.py:235
  219.5 7.6 %convert_reduce_fusion.5 = (f32[3,64]{1,0:T(4,128)}, bf16[3,64,512]{2,1,0:T(8,128)(2,1)}) fusion(bf16[512,3,64]{0,2,1:T(8,128)(2,1)S(1)} %bitcast.331, f32[3,512,512]{1,2,0:T(8,128)} %fusion.183, f32[3,512,512]{1,2,0:T(8,128)} %copy-done.8, f32[3,512]{1,0:T(4,128)} %log_add_fusion), kind=kOutput, calls=%fused_computation.236 | convolution fusion | flops 106465088 | bytes 6691584 | tf_op jit(solution)/shard_map/hqk,khe->qhe/dot_general | solution.py:234
  228.5 3.4 fusion.182
  231.9 7.1 %fusion.147 = bf16[3,64,512]{2,1,0:T(8,128)(2,1)} fusion(f32[3,512,512]{1,2,0:T(8,128)} %fusion.182, f32[3,512,512]{1,2,0:T(8,128)} %copy-done.6, f32[3,512]{1,0:T(4,128)S(1)} %log_add_fusion.1, f32[512,3,64]{0,2,1:T(8,128)} %bitcast.313, f32[3,64]{1,0:T(4,128)} %copy-done.98), kind=kOutput, calls=%fused_computation.216 | convolution fusion | flops 106465280 | bytes 6888192 | tf_op jit(solution)/shard_map/hqk,qhe->khe/dot_general | solution.py:235
  239.0 7.5 %convert_reduce_fusion.7 = (f32[3,64]{1,0:T(4,128)}, bf16[3,64,512]{2,1,0:T(8,128)(2,1)}) fusion(bf16[512,3,64]{0,2,1:T(8,128)(2,1)} %bitcast.327, f32[3,512,512]{1,2,0:T(8,128)} %fusion.182, f32[3,512,512]{1,2,0:T(8,128)} %copy-done.6, f32[3,512]{1,0:T(4,128)S(1)} %log_add_fusion.1), kind=kOutput, calls=%fused_computation.238 | convolution fusion | flops 106465088 | bytes 6691584 | tf_op jit(solution)/shard_map/hqk,khe->qhe/dot_general | solution.py:234
  246.5 3.8 convert_reduce_fusion.6
  250.8 2.4 fusion.180
  253.2 7.4 %fusion.159 = bf16[3,64,512]{2,1,0:T(8,128)(2,1)} fusion(f32[3,512,512]{1,2,0:T(8,128)} %fusion.180, f32[3,512,512]{1,2,0:T(8,128)} %copy-done.5, f32[3,512]{1,0:T(4,128)S(1)} %log_add_fusion.3, f32[512,3,64]{0,2,1:T(8,128)} %bitcast.309, f32[3,64]{1,0:T(4,128)S(1)} %copy-done.97), kind=kOutput, calls=%fused_computation.220 | convolution fusion | flops 106465280 | bytes 6888192 | tf_op jit(solution)/shard_map/hqk,qhe->khe/dot_general | solution.py:235
  260.7 7.1 %convert_reduce_fusion.11 = (f32[3,64]{1,0:T(4,128)S(1)}, bf16[3,64,512]{2,1,0:T(8,128)(2,1)}) fusion(bf16[512,3,64]{0,2,1:T(8,128)(2,1)} %bitcast.325, f32[3,512,512]{1,2,0:T(8,128)} %fusion.180, f32[3,512,512]{1,2,0:T(8,128)} %copy-done.5, f32[3,512]{1,0:T(4,128)S(1)} %log_add_fusion.3), kind=kOutput, calls=%fused_computation.242 | convolution fusion | flops 106465088 | bytes 6691584 | tf_op jit(solution)/shard_map/hqk,khe->qhe/dot_general | solution.py:234
  267.8 2.7 convert_reduce_fusion.10
  281.9 2.2 add_convert_fusion.4
  284.1 3.0 convolution_convert_fusion
  287.5 1.8 convolution_convert_fusion.1
  289.5 1.8 convolution_convert_fusion.2
  311.2 2.1 add_convert_fusion.1
  313.3 2.0 collective-permute-start.17
  316.7 2.0 collective-permute-start.20
  318.6 2.1 add_convert_fusion.3
  320.7 63.0 %collective-permute-done.20 = bf16[192,768]{1,0:T(8,128)(2,1)S(1)} collective-permute-done((bf16[192,768]{1,0:T(8,128)(2,1)S(1)}, bf16[192,768]{1,0:T(8,128)(2,1)S(1)}, u32[]{:S(2)}, u32[]{:S(2)}) %collective-permute-start.20) | collective-permute-done | bytes 294944 | tf_op jit(solution)/shard_map/ppermute | solution.py:38
  383.7 1.7 collective-permute-start.23
  387.9 2.7 add_convert_fusion
  390.6 21.5 %collective-permute-done.23 = bf16[768,768]{1,0:T(8,128)(2,1)S(1)} collective-permute-done((bf16[768,768]{1,0:T(8,128)(2,1)S(1)}, bf16[768,768]{1,0:T(8,128)(2,1)S(1)}, u32[]{:S(2)}, u32[]{:S(2)}) %collective-permute-start.23) | collective-permute-done | bytes 1179680 | tf_op jit(solution)/shard_map/ppermute | solution.py:38
  415.4 46.4 %all-reduce = (f32[4,1,1152]{2,1,0:T(1,128)S(1)}, f32[6,768]{1,0:T(8,128)S(1)}) all-reduce(f32[4,1,1152]{2,1,0:T(1,128)S(1)} %reshape_dynamic-update-slice_fusion, f32[6,768]{1,0:T(8,128)S(1)} %stack.99), channel_id=1, replica_groups=mesh['dp'=8,'mp'=4] {'dp','mp'}, use_global_device_ids=true, to_apply=%region_35.36 | all-reduce | flops 9216 | bytes 73728 | tf_op jit(solution)/shard_map/psum | solution.py:370
  463.8 5.1 convert_element_type.557
  468.9 86.9 %all-reduce.4.cloned.1.call-done = (bf16[3,768,192]{1,2,0:T(8,128)(2,1)}, bf16[192,768]{1,0:T(8,128)(2,1)}, bf16[768,768]{1,0:T(8,128)(2,1)}, bf16[768,768]{1,0:T(8,128)(2,1)}) async-done(((bf16[3,768,192]{1,2,0:T(8,128)(2,1)}, bf16[192,768]{1,0:T(8,128)(2,1)}, bf16[768,768]{1,0:T(8,128)(2,1)}, bf16[768,768]{1,0:T(8,128)(2,1)}), (bf16[3,768,192]{1,2,0:T(8,128)(2,1)}, bf16[192,768]{1,0:T(8,128)(2,1)}, ...) | async-done | bytes 3538960 | tf_op jit(solution)/shard_map/psum | solution.py:360
  555.9 2.9 convert_element_type.591
  (501 shorter events, 99.9 us)
Async XLA Ops:
  8.0 455.8 %all-gather.5.cloned.1.call-start = ((), (), s32[]{:S(2)}) async-start(), calls=%async_computation.1 | async-start | bytes 3932160 | tf_op jit(solution)/shard_map/all_gather | solution.py:357
  8.1 27.4 %collective-permute-start = (bf16[3,768,192]{1,2,0:T(8,128)(2,1)}, bf16[3,768,192]{1,2,0:T(8,128)(2,1)}, u32[]{:S(2)}, u32[]{:S(2)}) collective-permute-start(bf16[3,768,192]{1,2,0:T(8,128)(2,1)} %param.20), channel_id=1, source_target_pairs={{0,1},{1,0},{2,3},{3,2},{4,5},{5,4},{6,7},{7,6},{8,9},{9,8},{10,11... | collective-permute-start | bytes 2654216 | tf_op jit(solution)/shard_map/ppermute | solution.py:38
  8.6 28.9 %collective-permute-start.3 = (bf16[3,768,192]{1,2,0:T(8,128)(2,1)}, bf16[3,768,192]{1,2,0:T(8,128)(2,1)}, u32[]{:S(2)}, u32[]{:S(2)}) collective-permute-start(bf16[3,768,192]{1,2,0:T(8,128)(2,1)} %param.20), channel_id=1, source_target_pairs={{0,2},{1,3},{2,0},{3,1},{4,6},{5,7},{6,4},{7,5},{8,10},{9,11},{10,... | collective-permute-start | bytes 2654216 | tf_op jit(solution)/shard_map/ppermute | solution.py:38
  12.7 10.7 %collective-permute-start.1 = (f32[1,1152]{1,0:T(1,128)S(1)}, f32[1,1152]{1,0:T(1,128)S(1)}, u32[]{:S(2)}, u32[]{:S(2)}) collective-permute-start(f32[1,1152]{1,0:T(1,128)S(1)} %broadcast_in_dim.54), channel_id=1, source_target_pairs={{0,1},{1,0},{2,3},{3,2},{4,5},{5,4},{6,7},{7,6},{8,9},{9,8},{10,11... | collective-permute-start | bytes 13832 | tf_op jit(solution)/shard_map/ppermute | solution.py:38
  12.9 19.1 %collective-permute-start.4 = (f32[1,1152]{1,0:T(1,128)S(1)}, f32[1,1152]{1,0:T(1,128)S(1)}, u32[]{:S(2)}, u32[]{:S(2)}) collective-permute-start(f32[1,1152]{1,0:T(1,128)S(1)} %broadcast_in_dim.54), channel_id=1, source_target_pairs={{0,2},{1,3},{2,0},{3,1},{4,6},{5,7},{6,4},{7,5},{8,10},{9,11},{10,... | collective-permute-start | bytes 13832 | tf_op jit(solution)/shard_map/ppermute | solution.py:38
  13.2 31.8 %collective-permute-start.2 = (bf16[192,768]{1,0:T(8,128)(2,1)}, bf16[192,768]{1,0:T(8,128)(2,1)}, u32[]{:S(2)}, u32[]{:S(2)}) collective-permute-start(bf16[192,768]{1,0:T(8,128)(2,1)} %param.22), channel_id=1, source_target_pairs={{0,1},{1,0},{2,3},{3,2},{4,5},{5,4},{6,7},{7,6},{8,9},{9,8},{10,11... | collective-permute-start | bytes 884744 | tf_op jit(solution)/shard_map/ppermute | solution.py:38
  19.4 16.2 %copy-start = (bf16[2048,768]{1,0:T(8,128)(2,1)S(1)}, bf16[2048,768]{1,0:T(8,128)(2,1)}, u32[]{:S(2)}) copy-start(bf16[2048,768]{1,0:T(8,128)(2,1)} %param.18) | copy-start | bytes 9437188
  23.4 23.5 %collective-permute-start.5 = (bf16[192,768]{1,0:T(8,128)(2,1)}, bf16[192,768]{1,0:T(8,128)(2,1)}, u32[]{:S(2)}, u32[]{:S(2)}) collective-permute-start(bf16[192,768]{1,0:T(8,128)(2,1)} %param.22), channel_id=1, source_target_pairs={{0,2},{1,3},{2,0},{3,1},{4,6},{5,7},{6,4},{7,5},{8,10},{9,11},{10,... | collective-permute-start | bytes 884744 | tf_op jit(solution)/shard_map/ppermute | solution.py:38
  32.0 1.2 collective-permute-start.7
  32.3 7.4 %copy-start.100 = (f32[3,64]{1,0:T(4,128)}, f32[3,64]{1,0:T(4,128)S(1)}, u32[]{:S(2)}) copy-start(f32[3,64]{1,0:T(4,128)S(1)} %add.360) | copy-start | bytes 2308
  32.5 8.6 %copy-start.98 = (f32[3,64]{1,0:T(4,128)}, f32[3,64]{1,0:T(4,128)S(1)}, u32[]{:S(2)}) copy-start(f32[3,64]{1,0:T(4,128)S(1)} %add.367) | copy-start | bytes 2308
  32.6 10.5 %copy-start.106 = (f32[3,64]{1,0:T(4,128)}, f32[3,64]{1,0:T(4,128)S(1)}, u32[]{:S(2)}) copy-start(f32[3,64]{1,0:T(4,128)S(1)} %add.364) | copy-start | bytes 2308
  33.2 30.5 %collective-permute-start.11 = (bf16[768,768]{1,0:T(8,128)(2,1)}, bf16[768,768]{1,0:T(8,128)(2,1)}, u32[]{:S(2)}, u32[]{:S(2)}) collective-permute-start(bf16[768,768]{1,0:T(8,128)(2,1)} %param.26), channel_id=1, source_target_pairs={{0,2},{1,3},{2,0},{3,1},{4,6},{5,7},{6,4},{7,5},{8,10},{9,11},{10,... | collective-permute-start | bytes 3538952 | tf_op jit(solution)/shard_map/ppermute | solution.py:38
  35.4 54.6 %copy-start.99 = (f32[3,64]{1,0:T(4,128)}, f32[3,64]{1,0:T(4,128)S(1)}, u32[]{:S(2)}) copy-start(f32[3,64]{1,0:T(4,128)S(1)} %add.374) | copy-start | bytes 2308
  35.5 55.8 %copy-start.107 = (f32[3,64]{1,0:T(4,128)}, f32[3,64]{1,0:T(4,128)S(1)}, u32[]{:S(2)}) copy-start(f32[3,64]{1,0:T(4,128)S(1)} %add.371) | copy-start | bytes 2308
  35.5 53.1 %collective-permute-start.12 = (bf16[768,768]{1,0:T(8,128)(2,1)}, bf16[768,768]{1,0:T(8,128)(2,1)S(1)}, u32[]{:S(2)}, u32[]{:S(2)}) collective-permute-start(bf16[768,768]{1,0:T(8,128)(2,1)} %param.28), channel_id=1, source_target_pairs={{0,2},{1,3},{2,0},{3,1},{4,6},{5,7},{6,4},{7,5},{8,10},{9,11},{10,... | collective-permute-start | bytes 3538952 | tf_op jit(solution)/shard_map/ppermute | solution.py:38
  44.2 44.4 %collective-permute-start.6 = (bf16[3,768,192]{1,2,0:T(8,128)(2,1)}, bf16[3,768,192]{1,2,0:T(8,128)(2,1)S(1)}, u32[]{:S(2)}, u32[]{:S(2)}) collective-permute-start(bf16[3,768,192]{1,2,0:T(8,128)(2,1)} %collective-permute-done.3), channel_id=1, source_target_pairs={{0,1},{1,0},{2,3},{3,2},{4,5},{5,4},{6,7},{7,6},{8,9},{9,8},{10,11... | collective-permute-start | bytes 2654216 | tf_op jit(solution)/shard_map/ppermute | solution.py:38
  45.0 63.1 %collective-permute-start.9 = (bf16[768,768]{1,0:T(8,128)(2,1)S(1)}, bf16[768,768]{1,0:T(8,128)(2,1)S(1)}, u32[]{:S(2)}, u32[]{:S(2)}) collective-permute-start(bf16[768,768]{1,0:T(8,128)(2,1)S(1)} %copy-done.124), channel_id=1, source_target_pairs={{0,1},{1,0},{2,3},{3,2},{4,5},{5,4},{6,7},{7,6},{8,9},{9,8},{10,11... | collective-permute-start | bytes 3538952 | tf_op jit(solution)/shard_map/ppermute | solution.py:38
  46.9 68.3 %collective-permute-start.10 = (bf16[768,768]{1,0:T(8,128)(2,1)S(1)}, bf16[768,768]{1,0:T(8,128)(2,1)S(1)}, u32[]{:S(2)}, u32[]{:S(2)}) collective-permute-start(bf16[768,768]{1,0:T(8,128)(2,1)S(1)} %copy-done.122), channel_id=1, source_target_pairs={{0,1},{1,0},{2,3},{3,2},{4,5},{5,4},{6,7},{7,6},{8,9},{9,8},{10,11... | collective-permute-start | bytes 3538952 | tf_op jit(solution)/shard_map/ppermute | solution.py:38
  63.7 29.4 %collective-permute-start.8 = (bf16[192,768]{1,0:T(8,128)(2,1)}, bf16[192,768]{1,0:T(8,128)(2,1)S(1)}, u32[]{:S(2)}, u32[]{:S(2)}) collective-permute-start(bf16[192,768]{1,0:T(8,128)(2,1)} %collective-permute-done.5), channel_id=1, source_target_pairs={{0,1},{1,0},{2,3},{3,2},{4,5},{5,4},{6,7},{7,6},{8,9},{9,8},{10,11... | collective-permute-start | bytes 884744 | tf_op jit(solution)/shard_map/ppermute | solution.py:38
  88.6 25.8 %copy-start.126 = (bf16[768,768]{1,0:T(8,128)(2,1)}, bf16[768,768]{1,0:T(8,128)(2,1)S(1)}, u32[]{:S(2)}) copy-start(bf16[768,768]{1,0:T(8,128)(2,1)S(1)} %collective-permute-done.12) | copy-start | bytes 3538948
  88.6 28.2 %collective-permute-start.13 = (bf16[768,768]{1,0:T(8,128)(2,1)}, bf16[768,768]{1,0:T(8,128)(2,1)S(1)}, u32[]{:S(2)}, u32[]{:S(2)}) collective-permute-start(bf16[768,768]{1,0:T(8,128)(2,1)} %collective-permute-done.11), channel_id=1, source_target_pairs={{0,1},{1,0},{2,3},{3,2},{4,5},{5,4},{6,7},{7,6},{8,9},{9,8},{10,11... | collective-permute-start | bytes 3538952 | tf_op jit(solution)/shard_map/ppermute | solution.py:38
  88.6 33.9 %collective-permute-start.14 = (bf16[768,768]{1,0:T(8,128)(2,1)S(1)}, bf16[768,768]{1,0:T(8,128)(2,1)S(1)}, u32[]{:S(2)}, u32[]{:S(2)}) collective-permute-start(bf16[768,768]{1,0:T(8,128)(2,1)S(1)} %collective-permute-done.12), channel_id=1, source_target_pairs={{0,1},{1,0},{2,3},{3,2},{4,5},{5,4},{6,7},{7,6},{8,9},{9,8},{10,11... | collective-permute-start | bytes 3538952 | tf_op jit(solution)/shard_map/ppermute | solution.py:38
  94.8 27.7 %copy-start.3 = (f32[512,768]{1,0:T(8,128)}, f32[512,768]{1,0:T(8,128)S(1)}, u32[]{:S(2)}) copy-start(f32[512,768]{1,0:T(8,128)S(1)} %get-tuple-element.79) | copy-start | bytes 4718596
  95.9 21.0 %copy-start.12 = (bf16[512,768]{1,0:T(8,128)(2,1)}, bf16[512,768]{1,0:T(8,128)(2,1)S(1)}, u32[]{:S(2)}) copy-start(bf16[512,768]{1,0:T(8,128)(2,1)S(1)} %fusion.115) | copy-start | bytes 2359300
  101.4 12.2 %copy-start.19 = (bf16[512,768]{1,0:T(8,128)(2,1)}, bf16[512,768]{1,0:T(8,128)(2,1)S(1)}, u32[]{:S(2)}) copy-start(bf16[512,768]{1,0:T(8,128)(2,1)S(1)} %get-tuple-element.58) | copy-start | bytes 2359300
  108.1 6.3 %copy-start.132 = (bf16[512,768]{1,0:T(8,128)(2,1)}, bf16[512,768]{1,0:T(8,128)(2,1)S(1)}, u32[]{:S(2)}) copy-start(bf16[512,768]{1,0:T(8,128)(2,1)S(1)} %get-tuple-element.60) | copy-start | bytes 2359300
  116.9 5.7 copy-start.110
  116.9 5.6 copy-start.45
  124.8 38.1 %copy-start.10 = (bf16[512,768]{1,0:T(8,128)(2,1)}, bf16[512,768]{1,0:T(8,128)(2,1)S(1)}, u32[]{:S(2)}) copy-start(bf16[512,768]{1,0:T(8,128)(2,1)S(1)} %add_convert_fusion.5) | copy-start | bytes 2359300
  189.5 7.1 %copy-start.53 = (bf16[1,512,192]{1,2,0:T(8,128)(2,1)S(1)}, bf16[1,512,192]{1,2,0:T(8,128)(2,1)}, u32[]{:S(2)}) copy-start(bf16[1,512,192]{1,2,0:T(8,128)(2,1)} %copy-done.52) | copy-start | bytes 589828
  212.4 7.1 %copy-start.55 = (bf16[1,512,192]{1,2,0:T(8,128)(2,1)S(1)}, bf16[1,512,192]{1,2,0:T(8,128)(2,1)}, u32[]{:S(2)}) copy-start(bf16[1,512,192]{1,2,0:T(8,128)(2,1)} %copy-done.54) | copy-start | bytes 589828
  284.1 184.8 %all-gather.3.cloned.1.call-start = ((), (), s32[]{:S(2)}) async-start(), calls=%async_computation | async-start | bytes 3932160 | tf_op jit(solution)/shard_map/all_gather | solution.py:318
  287.2 23.6 %collective-permute-start.25 = (bf16[768,768]{1,0:T(8,128)(2,1)}, bf16[768,768]{1,0:T(8,128)(2,1)}, u32[]{:S(2)}, u32[]{:S(2)}) collective-permute-start(bf16[768,768]{1,0:T(8,128)(2,1)} %convolution_convert_fusion), channel_id=1, source_target_pairs={{0,1},{1,0},{2,3},{3,2},{4,5},{5,4},{6,7},{7,6},{8,9},{9,8},{10,11... | collective-permute-start | bytes 3538952 | tf_op jit(solution)/shard_map/ppermute | solution.py:38
  289.3 98.6 %collective-permute-start.24 = (bf16[768,768]{1,0:T(8,128)(2,1)}, bf16[768,768]{1,0:T(8,128)(2,1)}, u32[]{:S(2)}, u32[]{:S(2)}) collective-permute-start(bf16[768,768]{1,0:T(8,128)(2,1)} %convolution_convert_fusion.1), channel_id=1, source_target_pairs={{0,1},{1,0},{2,3},{3,2},{4,5},{5,4},{6,7},{7,6},{8,9},{9,8},{10,11... | collective-permute-start | bytes 3538952 | tf_op jit(solution)/shard_map/ppermute | solution.py:38
  291.3 25.3 %collective-permute-start.22 = (bf16[768,768]{1,0:T(8,128)(2,1)}, bf16[768,768]{1,0:T(8,128)(2,1)}, u32[]{:S(2)}, u32[]{:S(2)}) collective-permute-start(bf16[768,768]{1,0:T(8,128)(2,1)} %convolution_convert_fusion.2), channel_id=1, source_target_pairs={{0,1},{1,0},{2,3},{3,2},{4,5},{5,4},{6,7},{7,6},{8,9},{9,8},{10,11... | collective-permute-start | bytes 3538952 | tf_op jit(solution)/shard_map/ppermute | solution.py:38
  292.7 20.5 %collective-permute-start.19 = (bf16[192,768]{1,0:T(8,128)(2,1)}, bf16[192,768]{1,0:T(8,128)(2,1)}, u32[]{:S(2)}, u32[]{:S(2)}) collective-permute-start(bf16[192,768]{1,0:T(8,128)(2,1)} %convolution_convert_fusion.10), channel_id=1, source_target_pairs={{0,1},{1,0},{2,3},{3,2},{4,5},{5,4},{6,7},{7,6},{8,9},{9,8},{10,11... | collective-permute-start | bytes 884744 | tf_op jit(solution)/shard_map/ppermute | solution.py:38
  295.0 14.0 %collective-permute-start.16 = (bf16[3,768,192]{1,2,0:T(8,128)(2,1)}, bf16[3,768,192]{1,2,0:T(8,128)(2,1)}, u32[]{:S(2)}, u32[]{:S(2)}) collective-permute-start(bf16[3,768,192]{1,2,0:T(8,128)(2,1)} %pad_maximum_fusion.1), channel_id=1, source_target_pairs={{0,1},{1,0},{2,3},{3,2},{4,5},{5,4},{6,7},{7,6},{8,9},{9,8},{10,11... | collective-permute-start | bytes 2654216 | tf_op jit(solution)/shard_map/ppermute | solution.py:38
  299.6 256.2 %all-reduce.4.cloned.1.call-start = ((), (), s32[]{:S(2)}) async-start(), calls=%async_computation.2 | async-start | bytes 7077888 | tf_op jit(solution)/shard_map/psum | solution.py:360
  309.0 6.2 %collective-permute-start.18 = (bf16[192,768]{1,0:T(8,128)(2,1)S(1)}, bf16[192,768]{1,0:T(8,128)(2,1)S(1)}, u32[]{:S(2)}, u32[]{:S(2)}) collective-permute-start(bf16[192,768]{1,0:T(8,128)(2,1)S(1)} %convolution_convert_fusion.11), channel_id=1, source_target_pairs={{0,1},{1,0},{2,3},{3,2},{4,5},{5,4},{6,7},{7,6},{8,9},{9,8},{10,11... | collective-permute-start | bytes 884744 | tf_op jit(solution)/shard_map/ppermute | solution.py:38
  310.8 7.9 %copy-start.135 = (bf16[512,768]{1,0:T(8,128)(2,1)S(1)}, bf16[512,768]{1,0:T(8,128)(2,1)}, u32[]{:S(2)}) copy-start(bf16[512,768]{1,0:T(8,128)(2,1)} %copy-done.134) | copy-start | bytes 2359300
  310.8 73.0 %collective-permute-start.15 = (bf16[3,768,192]{1,2,0:T(8,128)(2,1)S(1)}, bf16[3,768,192]{1,2,0:T(8,128)(2,1)S(1)}, u32[]{:S(2)}, u32[]{:S(2)}) collective-permute-start(bf16[3,768,192]{1,2,0:T(8,128)(2,1)S(1)} %pad_maximum_fusion), channel_id=1, source_target_pairs={{0,1},{1,0},{2,3},{3,2},{4,5},{5,4},{6,7},{7,6},{8,9},{9,8},{10,11... | collective-permute-start | bytes 2654216 | tf_op jit(solution)/shard_map/ppermute | solution.py:38
  313.3 73.4 %collective-permute-start.17 = (bf16[3,768,192]{1,2,0:T(8,128)(2,1)S(1)}, bf16[3,768,192]{1,2,0:T(8,128)(2,1)S(1)}, u32[]{:S(2)}, u32[]{:S(2)}) collective-permute-start(bf16[3,768,192]{1,2,0:T(8,128)(2,1)S(1)} %fusion.50), channel_id=1, source_target_pairs={{0,2},{1,3},{2,0},{3,1},{4,6},{5,7},{6,4},{7,5},{8,10},{9,11},{10,... | collective-permute-start | bytes 2654216 | tf_op jit(solution)/shard_map/ppermute | solution.py:38
  315.2 72.7 %collective-permute-start.26 = (bf16[768,768]{1,0:T(8,128)(2,1)S(1)}, bf16[768,768]{1,0:T(8,128)(2,1)S(1)}, u32[]{:S(2)}, u32[]{:S(2)}) collective-permute-start(bf16[768,768]{1,0:T(8,128)(2,1)S(1)} %add_convert_fusion.1), channel_id=1, source_target_pairs={{0,2},{1,3},{2,0},{3,1},{4,6},{5,7},{6,4},{7,5},{8,10},{9,11},{10,... | collective-permute-start | bytes 3538952 | tf_op jit(solution)/shard_map/ppermute | solution.py:38
  316.6 68.8 %copy-start.59 = (bf16[3,64,512]{2,1,0:T(8,128)(2,1)S(1)}, bf16[3,64,512]{2,1,0:T(8,128)(2,1)}, u32[]{:S(2)}) copy-start(bf16[3,64,512]{2,1,0:T(8,128)(2,1)} %copy-done.58) | copy-start | bytes 589828
  316.7 67.1 %collective-permute-start.20 = (bf16[192,768]{1,0:T(8,128)(2,1)S(1)}, bf16[192,768]{1,0:T(8,128)(2,1)S(1)}, u32[]{:S(2)}, u32[]{:S(2)}) collective-permute-start(bf16[192,768]{1,0:T(8,128)(2,1)S(1)} %add_convert_fusion.7), channel_id=1, source_target_pairs={{0,2},{1,3},{2,0},{3,1},{4,6},{5,7},{6,4},{7,5},{8,10},{9,11},{10,... | collective-permute-start | bytes 884744 | tf_op jit(solution)/shard_map/ppermute | solution.py:38
  383.7 6.9 %collective-permute-start.21 = (bf16[768,768]{1,0:T(8,128)(2,1)S(1)}, bf16[768,768]{1,0:T(8,128)(2,1)S(1)}, u32[]{:S(2)}, u32[]{:S(2)}) collective-permute-start(bf16[768,768]{1,0:T(8,128)(2,1)S(1)} %convolution_convert_fusion.3), channel_id=1, source_target_pairs={{0,1},{1,0},{2,3},{3,2},{4,5},{5,4},{6,7},{7,6},{8,9},{9,8},{10,11... | collective-permute-start | bytes 3538952 | tf_op jit(solution)/shard_map/ppermute | solution.py:38
  383.7 28.4 %collective-permute-start.23 = (bf16[768,768]{1,0:T(8,128)(2,1)S(1)}, bf16[768,768]{1,0:T(8,128)(2,1)S(1)}, u32[]{:S(2)}, u32[]{:S(2)}) collective-permute-start(bf16[768,768]{1,0:T(8,128)(2,1)S(1)} %add_convert_fusion.3), channel_id=1, source_target_pairs={{0,2},{1,3},{2,0},{3,1},{4,6},{5,7},{6,4},{7,5},{8,10},{9,11},{10,... | collective-permute-start | bytes 3538952 | tf_op jit(solution)/shard_map/ppermute | solution.py:38
  (130 other events, 250.6 us)
Sparse Core Ops, SparseCore 0:
  284.2 31.1 all-gather.4
  317.0 45.5 all-gather.2
Sparse Core Ops, SparseCore 1:
  413.8 142.0 all-reduce.3
